TPU v7x, 128 devices: a whole 4x4x4 slice. The times are simulated.
128 devices in a mesh: ctx: 64 (over y_hi, z, x, core), head: 2 (over y_lo).
Axes of the slice: x: 4, y: 4 (y_hi: 2, y_lo: 2; y = y_hi * 2 + y_lo), z: 4, core: 2. Of those that a mesh axis runs over, the one named last changes fastest.
Arguments:
- queries: bfloat16 [16384, 8192], P('ctx', 'head'), may hold values from -5 to 5
- keys: bfloat16 [16384, 512], P(('ctx', 'head')), may hold values from -5 to 5
- values: bfloat16 [16384, 512], P(('ctx', 'head')), may hold values from -6 to 6
- d_out: bfloat16 [16384, 8192], P('ctx', 'head'), may hold values from -6 to 6
- selected: int32 [256, 12], P('ctx'), may hold values from 0 to 11, as said below
- partners: int32 [2, 64], replicated, may hold values from 0 to 63, as said below
Outputs:
- attended: bfloat16 [16384, 8192], P('ctx', 'head')
- grad_queries: bfloat16 [16384, 8192], P('ctx', 'head')
- grad_keys: bfloat16 [16384, 512], P(('ctx', 'head'))
- grad_values: bfloat16 [16384, 512], P(('ctx', 'head'))
Inputs may be any that keep to these rules, and one draw needn't show every extreme that they name: `selected`: row b lists 12 different candidate blocks of query block b: 0 to 3 are its own shard's key blocks, 4 to 7 those of its partner under the first matching, 8 to 11 those under the second; the first entry is the query block's own key block (b modulo 4). `partners`: row r gives for every shard i its partner i XOR m_r, with a mask m_r that is the same for all shards; one of the two masks is 32, the other is 2 ** j - 1 for some j of 1 to 6, and either may stand in either row.
All inputs are finite; a program needn't handle non-finite values.
Results may differ from a plain program's by a relative error of at most 0.018.
Values may be sent and summed in bfloat16 or wider, within the bound.
No kernel may reach another device: no remote copies, remote signals or barrier semaphores. Data moves between devices by JAX's collectives and lax.ppermute only.
A program may use at most 128 MiB of HBM per device.

v0:
```python
import jax
import jax.numpy as jnp
from jax import lax
from jax.sharding import PartitionSpec as P

HQ = 64
KVH = 4
DH = 128
BLK = 64
SEL = 12


def from_partner(value, axis, distance):
    mask = 2**distance
    pairs = [(source, source ^ mask) for source in range(lax.axis_size(axis))]
    return lax.ppermute(value, axis, pairs)


def keep_or_take(current, arrived, mask_value, bit_number):
    bit_set = mask_value // 2**bit_number % 2 == 1
    return tuple(
        (jnp.where(bit_set, new_part, old_part) for old_part, new_part in zip(current, arrived))
    )


def return_pairs(pair_first, pair_second, mask_first, mask_second, bit_total):
    for bit_number in range(bit_total):
        swapped = from_partner(
            (pair_first[0], pair_first[1], pair_second[0], pair_second[1]), "ctx", bit_number
        )
        pair_first = keep_or_take(pair_first, swapped[0:2], mask_first, bit_number)
        pair_second = keep_or_take(pair_second, swapped[2:4], mask_second, bit_number)
    return (pair_first, pair_second)


def body(queries, keys, values, d_out, selected, partners):
    head_count = lax.axis_size("head")
    kv_local = KVH // head_count
    group_size = HQ // KVH
    tokens_dev = queries.shape[0]
    query_width = queries.shape[1]
    block_count = tokens_dev // BLK
    cand_blocks = 3 * block_count
    kv_width = kv_local * DH
    score_scale = DH ** (-0.5)
    keys_local, values_local = (
        lax.all_to_all(keys, "head", split_axis=1, concat_axis=0, tiled=True),
        lax.all_to_all(values, "head", split_axis=1, concat_axis=0, tiled=True),
    )
    mask_first = partners[0, 0]
    mask_second = partners[1, 0]
    bit_total = lax.axis_size("ctx").bit_length() - 1
    every_key, every_value = (
        lax.all_gather(keys_local, "ctx", axis=0, tiled=True),
        lax.all_gather(values_local, "ctx", axis=0, tiled=True),
    )
    own_index = lax.axis_index("ctx")

    def shard_rows(source, mask_value):
        row_start = jnp.bitwise_xor(own_index, mask_value) * tokens_dev
        return lax.dynamic_slice_in_dim(source, row_start, tokens_dev, 0)

    pair_first = (shard_rows(every_key, mask_first), shard_rows(every_value, mask_first))
    pair_second = (shard_rows(every_key, mask_second), shard_rows(every_value, mask_second))
    cand_keys = jnp.concatenate([keys_local, pair_first[0], pair_second[0]], 0).reshape(
        cand_blocks, BLK, kv_local, DH
    )
    cand_values = jnp.concatenate([values_local, pair_first[1], pair_second[1]], 0).reshape(
        cand_blocks, BLK, kv_local, DH
    )
    cand_ids = jnp.arange(cand_blocks, dtype=jnp.int32)

    def one_block(block_index, loop_state):
        out_all, grad_q_all, key_terms, value_terms = loop_state
        row_start = block_index * BLK
        query_block = lax.dynamic_slice_in_dim(queries, row_start, BLK, 0).reshape(
            BLK, kv_local, group_size, DH
        )
        grad_block = lax.dynamic_slice_in_dim(d_out, row_start, BLK, 0).reshape(
            BLK, kv_local, group_size, DH
        )
        chosen = lax.dynamic_index_in_dim(selected, block_index, 0, keepdims=False)
        picked_keys = jnp.take(cand_keys, chosen, axis=0).reshape(SEL * BLK, kv_local, DH)
        picked_values = jnp.take(cand_values, chosen, axis=0).reshape(SEL * BLK, kv_local, DH)
        scores = (
            jnp.einsum(
                "qgrd,kgd->grqk", query_block, picked_keys, preferred_element_type=jnp.float32
            )
            * score_scale
        )
        row_max = jnp.max(scores, axis=-1, keepdims=True)
        exp_scores = jnp.exp(scores - row_max)
        prob_full = exp_scores / jnp.sum(exp_scores, axis=-1, keepdims=True)
        prob_low = prob_full.astype(jnp.bfloat16)
        out_block = jnp.einsum(
            "grqk,kgd->qgrd", prob_low, picked_values, preferred_element_type=jnp.float32
        ).astype(jnp.bfloat16)
        grad_p = jnp.einsum(
            "qgrd,kgd->grqk", grad_block, picked_values, preferred_element_type=jnp.float32
        )
        row_delta = jnp.einsum(
            "qgrd,qgrd->grq", grad_block, out_block, preferred_element_type=jnp.float32
        )
        grad_s = (prob_full * (grad_p - row_delta[..., None]) * score_scale).astype(jnp.bfloat16)
        grad_q = jnp.einsum(
            "grqk,kgd->qgrd", grad_s, picked_keys, preferred_element_type=jnp.float32
        ).astype(jnp.bfloat16)
        key_part = jnp.einsum(
            "grqk,qgrd->kgd", grad_s, query_block, preferred_element_type=jnp.float32
        ).reshape(SEL, BLK * kv_width)
        value_part = jnp.einsum(
            "grqk,qgrd->kgd", prob_low, grad_block, preferred_element_type=jnp.float32
        ).reshape(SEL, BLK * kv_width)
        one_hot = (chosen[:, None] == cand_ids[None, :]).astype(jnp.float32)
        key_terms = key_terms + jnp.dot(
            one_hot.T, key_part, precision=lax.Precision.HIGHEST, preferred_element_type=jnp.float32
        )
        value_terms = value_terms + jnp.dot(
            one_hot.T,
            value_part,
            precision=lax.Precision.HIGHEST,
            preferred_element_type=jnp.float32,
        )
        out_all = lax.dynamic_update_slice_in_dim(
            out_all, out_block.reshape(BLK, query_width), row_start, 0
        )
        grad_q_all = lax.dynamic_update_slice_in_dim(
            grad_q_all, grad_q.reshape(BLK, query_width), row_start, 0
        )
        return (out_all, grad_q_all, key_terms, value_terms)

    start_state = (
        jnp.zeros((tokens_dev, query_width), jnp.bfloat16),
        jnp.zeros((tokens_dev, query_width), jnp.bfloat16),
        jnp.zeros((cand_blocks, BLK * kv_width), jnp.float32),
        jnp.zeros((cand_blocks, BLK * kv_width), jnp.float32),
    )
    attended, grad_queries, key_terms, value_terms = lax.fori_loop(
        0, block_count, one_block, start_state
    )
    first_terms = (
        key_terms[block_count : 2 * block_count].astype(jnp.bfloat16),
        value_terms[block_count : 2 * block_count].astype(jnp.bfloat16),
    )
    second_terms = (
        key_terms[2 * block_count :].astype(jnp.bfloat16),
        value_terms[2 * block_count :].astype(jnp.bfloat16),
    )
    back_first, back_second = return_pairs(
        first_terms, second_terms, mask_first, mask_second, bit_total
    )
    key_total = (
        key_terms[:block_count]
        + back_first[0].astype(jnp.float32)
        + back_second[0].astype(jnp.float32)
    )
    value_total = (
        value_terms[:block_count]
        + back_first[1].astype(jnp.float32)
        + back_second[1].astype(jnp.float32)
    )
    key_rows = key_total.reshape(tokens_dev, kv_width).astype(jnp.bfloat16)
    value_rows = value_total.reshape(tokens_dev, kv_width).astype(jnp.bfloat16)
    grad_keys, grad_values = (
        lax.all_to_all(key_rows, "head", split_axis=0, concat_axis=1, tiled=True),
        lax.all_to_all(value_rows, "head", split_axis=0, concat_axis=1, tiled=True),
    )
    return (attended, grad_queries, grad_keys, grad_values)


def solution(mesh):
    return jax.shard_map(
        body,
        mesh=mesh,
        in_specs=(
            P("ctx", "head"),
            P(("ctx", "head"), None),
            P(("ctx", "head"), None),
            P("ctx", "head"),
            P("ctx", None),
            P(),
        ),
        out_specs=(
            P("ctx", "head"),
            P("ctx", "head"),
            P(("ctx", "head"), None),
            P(("ctx", "head"), None),
        ),
        check_vma=False,
    )
```

profile of v0, /device:TPU:0, one launch (start us, length us, event | category | flops | bytes accessed | tf_op | source)
XLA Modules:
  0.0 422.1 jit_solution(7663354984939706454)
XLA Ops:
  8.4 7.5 %all_to_all.70 = bf16[128,2,256]{2,0,1:T(8,128)(2,1)} all-to-all(bf16[128,2,256]{2,0,1:T(8,128)(2,1)S(1)} %copy.61), channel_id=1, replica_groups=mesh['ctx'=64,'head'=2] {'head'}, dimensions={1} | all-to-all | bytes 262144 | tf_op jit(solution)/shard_map/all_to_all | solution.py:47
  17.1 7.5 %all_to_all.71 = bf16[128,2,256]{2,0,1:T(8,128)(2,1)} all-to-all(bf16[128,2,256]{2,0,1:T(8,128)(2,1)S(1)} %copy.59), channel_id=1, replica_groups=mesh['ctx'=64,'head'=2] {'head'}, dimensions={1} | all-to-all | bytes 262144 | tf_op jit(solution)/shard_map/all_to_all | solution.py:48
  32.9 66.7 %all-gather.5.cloned.1.call-done = bf16[16384,256]{1,0:T(8,128)(2,1)} async-done(((bf16[256,256]{1,0:T(8,128)(2,1)}), bf16[16384,256]{1,0:T(8,128)(2,1)}) %all-gather.5.cloned.1.call-update) | async-done | bytes 8388624 | tf_op jit(solution)/shard_map/all_gather | solution.py:54
  99.6 81.9 %all-gather.3.cloned.1.call-done = bf16[16384,256]{1,0:T(8,128)(2,1)} async-done(((bf16[256,256]{1,0:T(8,128)(2,1)}), bf16[16384,256]{1,0:T(8,128)(2,1)}) %all-gather.3.cloned.1.call-update) | async-done | bytes 8388624 | tf_op jit(solution)/shard_map/all_gather | solution.py:55
  187.7 157.0 %while.20 = (s32[]{:T(128)}, bf16[256,4096]{1,0:T(8,128)(2,1)}, bf16[256,4096]{1,0:T(8,128)(2,1)}, f32[12,16384]{1,0:T(8,128)}, f32[12,16384]{1,0:T(8,128)}, /*i...) while((s32[]{:T(128)}, bf16[256,4096]{1,0:T(8,128)(2,1)}, ...), condition=%wide.region_3.5_spmd.clone, body=%wide.region_0.4_spmd.clone.sunk | while | flops 2491023616 | bytes 80786256 | solution.py:138
  188.4 2.3 gather_fusion.1
  195.4 4.7 %fusion.96 = (f32[2,16,64]{2,1,0:T(8,128)S(1)}, f32[2,16,64,768]{3,2,1,0:T(8,128)}) fusion(bf16[64,2,16,128]{3,2,1,0:T(8,128)(2,1)S(1)} %bitcast.140, bf16[768,2,128,1]{2,1,0,3:T(2,128)(2,1)S(1)} %bitcast.138), kind=kOutput, calls=%fused_computation.82.clone.1 | convolution fusion | flops 407372544 | bytes 7217152 | tf_op jit(solution)/shard_map/while/body/eval_jaxpr/sub | solution.py:92
  200.1 3.2 fusion.97
  203.3 2.2 multiply_reduce_fusion.2
  205.5 3.1 fusion.101
  210.1 3.6 fusion.98
  215.1 2.2 fusion.100
  225.8 2.3 gather_fusion.1
  232.8 4.7 %fusion.96 = (f32[2,16,64]{2,1,0:T(8,128)S(1)}, f32[2,16,64,768]{3,2,1,0:T(8,128)}) fusion(bf16[64,2,16,128]{3,2,1,0:T(8,128)(2,1)S(1)} %bitcast.140, bf16[768,2,128,1]{2,1,0,3:T(2,128)(2,1)S(1)} %bitcast.138), kind=kOutput, calls=%fused_computation.82.clone.1 | convolution fusion | flops 407372544 | bytes 7217152 | tf_op jit(solution)/shard_map/while/body/eval_jaxpr/sub | solution.py:92
  237.5 3.2 fusion.97
  240.7 2.2 multiply_reduce_fusion.2
  242.9 3.1 fusion.101
  247.5 3.6 fusion.98
  252.5 2.2 fusion.100
  257.0 2.9 convolution_add_fusion.4
  260.6 3.0 convolution_add_fusion.5
  265.6 2.3 gather_fusion.1
  272.6 4.7 %fusion.96 = (f32[2,16,64]{2,1,0:T(8,128)S(1)}, f32[2,16,64,768]{3,2,1,0:T(8,128)}) fusion(bf16[64,2,16,128]{3,2,1,0:T(8,128)(2,1)S(1)} %bitcast.140, bf16[768,2,128,1]{2,1,0,3:T(2,128)(2,1)S(1)} %bitcast.138), kind=kOutput, calls=%fused_computation.82.clone.1 | convolution fusion | flops 407372544 | bytes 7217152 | tf_op jit(solution)/shard_map/while/body/eval_jaxpr/sub | solution.py:92
  277.3 3.2 fusion.97
  280.6 2.2 multiply_reduce_fusion.2
  282.8 3.1 fusion.101
  287.3 3.6 fusion.98
  292.4 2.2 fusion.100
  296.9 2.9 convolution_add_fusion.4
  300.5 3.0 convolution_add_fusion.5
  305.5 2.3 gather_fusion.1
  312.5 4.7 %fusion.96 = (f32[2,16,64]{2,1,0:T(8,128)S(1)}, f32[2,16,64,768]{3,2,1,0:T(8,128)}) fusion(bf16[64,2,16,128]{3,2,1,0:T(8,128)(2,1)S(1)} %bitcast.140, bf16[768,2,128,1]{2,1,0,3:T(2,128)(2,1)S(1)} %bitcast.138), kind=kOutput, calls=%fused_computation.82.clone.1 | convolution fusion | flops 407372544 | bytes 7217152 | tf_op jit(solution)/shard_map/while/body/eval_jaxpr/sub | solution.py:92
  317.2 3.2 fusion.97
  322.7 3.1 fusion.101
  327.2 3.6 fusion.98
  332.2 2.2 fusion.100
  336.8 2.9 convolution_add_fusion.4
  340.3 3.0 convolution_add_fusion.5
  355.3 3.1 collective-permute-start.14
  358.5 2.7 collective-permute-start.20
  361.3 2.7 collective-permute-start.2
  364.1 2.7 collective-permute-start.8
  368.9 2.5 collective-permute-done.20
  371.7 2.5 collective-permute-done.2
  398.7 3.4 all-to-all-start.3
  404.0 2.5 all-to-all-done.3
  406.5 3.4 all-to-all-start.2
  410.8 3.6 all-to-all-done.2
  (215 shorter events, 106.1 us)
Async XLA Ops:
  7.2 92.4 %all-gather.5.cloned.1.call-start = ((), (), s32[]{:S(2)}) async-start(), calls=%async_computation.5 | async-start | bytes 8519680 | tf_op jit(solution)/shard_map/all_gather | solution.py:54
  15.9 165.5 %all-gather.3.cloned.1.call-start = ((), (), s32[]{:S(2)}) async-start(), calls=%async_computation.4 | async-start | bytes 8519680 | tf_op jit(solution)/shard_map/all_gather | solution.py:55
  24.6 159.8 %copy-start.6 = (bf16[128,2,256]{2,0,1:T(8,128)(2,1)S(1)}, bf16[128,2,256]{2,0,1:T(8,128)(2,1)}, u32[]{:S(2)}) copy-start(bf16[128,2,256]{2,0,1:T(8,128)(2,1)} %all_to_all.71) | copy-start | bytes 393220
  187.7 7.4 %copy-start.2 = (bf16[12,64,2,128]{3,2,1,0:T(2,128)(2,1)}, bf16[12,64,2,128]{3,2,1,0:T(2,128)(2,1)S(1)}, u32[]{:S(2)}) copy-start(bf16[12,64,2,128]{3,2,1,0:T(2,128)(2,1)S(1)} %get-tuple-element.396) | copy-start | bytes 1179652 | tf_op jit(solution)/shard_map/while
  195.2 4.9 %copy-start.4 = (bf16[8,8,32,128]{3,2,1,0:T(8,128)(2,1)}, bf16[8,8,32,128]{3,2,1,0:T(8,128)(2,1)S(1)}, u32[]{:S(2)}) copy-start(bf16[8,8,32,128]{3,2,1,0:T(8,128)(2,1)S(1)} %copy.158) | copy-start | bytes 1572868 | tf_op jit(solution)/shard_map/while
  210.1 3.7 copy-start.1
  222.0 3.1 copy-start.3
  225.0 7.4 %copy-start.2 = (bf16[12,64,2,128]{3,2,1,0:T(2,128)(2,1)}, bf16[12,64,2,128]{3,2,1,0:T(2,128)(2,1)S(1)}, u32[]{:S(2)}) copy-start(bf16[12,64,2,128]{3,2,1,0:T(2,128)(2,1)S(1)} %get-tuple-element.396) | copy-start | bytes 1179652 | tf_op jit(solution)/shard_map/while
  232.6 4.9 %copy-start.4 = (bf16[8,8,32,128]{3,2,1,0:T(8,128)(2,1)}, bf16[8,8,32,128]{3,2,1,0:T(8,128)(2,1)S(1)}, u32[]{:S(2)}) copy-start(bf16[8,8,32,128]{3,2,1,0:T(8,128)(2,1)S(1)} %copy.158) | copy-start | bytes 1572868 | tf_op jit(solution)/shard_map/while
  247.5 3.7 copy-start.1
  259.9 3.6 copy-start
  260.6 4.3 %copy-start.3 = (bf16[12,64,2,128]{3,2,1,0:T(2,128)(2,1)S(1)}, bf16[12,64,2,128]{3,2,1,0:T(2,128)(2,1)}, u32[]{:S(2)}) copy-start(bf16[12,64,2,128]{3,2,1,0:T(2,128)(2,1)} %copy-done.2) | copy-start | bytes 1179652 | tf_op jit(solution)/shard_map/while
  264.9 7.4 %copy-start.2 = (bf16[12,64,2,128]{3,2,1,0:T(2,128)(2,1)}, bf16[12,64,2,128]{3,2,1,0:T(2,128)(2,1)S(1)}, u32[]{:S(2)}) copy-start(bf16[12,64,2,128]{3,2,1,0:T(2,128)(2,1)S(1)} %get-tuple-element.396) | copy-start | bytes 1179652 | tf_op jit(solution)/shard_map/while
  272.5 4.9 %copy-start.4 = (bf16[8,8,32,128]{3,2,1,0:T(8,128)(2,1)}, bf16[8,8,32,128]{3,2,1,0:T(8,128)(2,1)S(1)}, u32[]{:S(2)}) copy-start(bf16[8,8,32,128]{3,2,1,0:T(8,128)(2,1)S(1)} %copy.158) | copy-start | bytes 1572868 | tf_op jit(solution)/shard_map/while
  287.3 3.7 copy-start.1
  299.8 3.6 copy-start
  300.5 4.3 %copy-start.3 = (bf16[12,64,2,128]{3,2,1,0:T(2,128)(2,1)S(1)}, bf16[12,64,2,128]{3,2,1,0:T(2,128)(2,1)}, u32[]{:S(2)}) copy-start(bf16[12,64,2,128]{3,2,1,0:T(2,128)(2,1)} %copy-done.2) | copy-start | bytes 1179652 | tf_op jit(solution)/shard_map/while
  304.8 7.4 %copy-start.2 = (bf16[12,64,2,128]{3,2,1,0:T(2,128)(2,1)}, bf16[12,64,2,128]{3,2,1,0:T(2,128)(2,1)S(1)}, u32[]{:S(2)}) copy-start(bf16[12,64,2,128]{3,2,1,0:T(2,128)(2,1)S(1)} %get-tuple-element.396) | copy-start | bytes 1179652 | tf_op jit(solution)/shard_map/while
  312.4 4.9 %copy-start.4 = (bf16[8,8,32,128]{3,2,1,0:T(8,128)(2,1)}, bf16[8,8,32,128]{3,2,1,0:T(8,128)(2,1)S(1)}, u32[]{:S(2)}) copy-start(bf16[8,8,32,128]{3,2,1,0:T(8,128)(2,1)S(1)} %copy.158) | copy-start | bytes 1572868 | tf_op jit(solution)/shard_map/while
  327.2 3.7 copy-start.1
  339.7 3.6 copy-start
  340.3 4.3 %copy-start.3 = (bf16[12,64,2,128]{3,2,1,0:T(2,128)(2,1)S(1)}, bf16[12,64,2,128]{3,2,1,0:T(2,128)(2,1)}, u32[]{:S(2)}) copy-start(bf16[12,64,2,128]{3,2,1,0:T(2,128)(2,1)} %copy-done.2) | copy-start | bytes 1179652 | tf_op jit(solution)/shard_map/while
  346.1 2.6 collective-permute-start.12
  346.4 2.3 collective-permute-start.18
  348.1 2.9 collective-permute-start
  348.4 2.6 collective-permute-start.6
  348.8 6.4 %collective-permute-start.13 = (bf16[4,16384]{1,0:T(4,128)(2,1)S(1)}, bf16[4,16384]{1,0:T(4,128)(2,1)S(1)}, u32[]{:S(2)}, u32[]{:S(2)}) collective-permute-start(bf16[4,16384]{1,0:T(4,128)(2,1)S(1)} %get-tuple-element.269), channel_id=1, source_target_pairs={{0,4},{2,6},{4,0},{6,2},{8,12},{10,14},{12,8},{14,10},{16,20},{18,... | collective-permute-start | bytes 393224 | tf_op jit(solution)/shard_map/ppermute | solution.py:16
  350.4 8.0 %collective-permute-start.19 = (bf16[4,16384]{1,0:T(4,128)(2,1)S(1)}, bf16[4,16384]{1,0:T(4,128)(2,1)S(1)}, u32[]{:S(2)}, u32[]{:S(2)}) collective-permute-start(bf16[4,16384]{1,0:T(4,128)(2,1)S(1)} %get-tuple-element.270), channel_id=1, source_target_pairs={{0,4},{2,6},{4,0},{6,2},{8,12},{10,14},{12,8},{14,10},{16,20},{18,... | collective-permute-start | bytes 393224 | tf_op jit(solution)/shard_map/ppermute | solution.py:16
  351.1 10.1 %collective-permute-start.1 = (bf16[4,16384]{1,0:T(4,128)(2,1)S(1)}, bf16[4,16384]{1,0:T(4,128)(2,1)S(1)}, u32[]{:S(2)}, u32[]{:S(2)}) collective-permute-start(bf16[4,16384]{1,0:T(4,128)(2,1)S(1)} %get-tuple-element.273), channel_id=1, source_target_pairs={{0,4},{2,6},{4,0},{6,2},{8,12},{10,14},{12,8},{14,10},{16,20},{18,... | collective-permute-start | bytes 393224 | tf_op jit(solution)/shard_map/ppermute | solution.py:16
  352.7 11.3 %collective-permute-start.7 = (bf16[4,16384]{1,0:T(4,128)(2,1)S(1)}, bf16[4,16384]{1,0:T(4,128)(2,1)S(1)}, u32[]{:S(2)}, u32[]{:S(2)}) collective-permute-start(bf16[4,16384]{1,0:T(4,128)(2,1)S(1)} %get-tuple-element.274), channel_id=1, source_target_pairs={{0,4},{2,6},{4,0},{6,2},{8,12},{10,14},{12,8},{14,10},{16,20},{18,... | collective-permute-start | bytes 393224 | tf_op jit(solution)/shard_map/ppermute | solution.py:16
  355.3 13.3 %collective-permute-start.14 = (bf16[4,16384]{1,0:T(4,128)(2,1)S(1)}, bf16[4,16384]{1,0:T(4,128)(2,1)S(1)}, u32[]{:S(2)}, u32[]{:S(2)}) collective-permute-start(bf16[4,16384]{1,0:T(4,128)(2,1)S(1)} %broadcast_select_fusion.14), channel_id=1, source_target_pairs={{0,8},{2,10},{4,12},{6,14},{8,0},{10,2},{12,4},{14,6},{16,24},{18,... | collective-permute-start | bytes 393224 | tf_op jit(solution)/shard_map/ppermute | solution.py:16
  358.5 13.0 %collective-permute-start.20 = (bf16[4,16384]{1,0:T(4,128)(2,1)S(1)}, bf16[4,16384]{1,0:T(4,128)(2,1)S(1)}, u32[]{:S(2)}, u32[]{:S(2)}) collective-permute-start(bf16[4,16384]{1,0:T(4,128)(2,1)S(1)} %broadcast_select_fusion.4), channel_id=1, source_target_pairs={{0,8},{2,10},{4,12},{6,14},{8,0},{10,2},{12,4},{14,6},{16,24},{18,... | collective-permute-start | bytes 393224 | tf_op jit(solution)/shard_map/ppermute | solution.py:16
  361.3 13.0 %collective-permute-start.2 = (bf16[4,16384]{1,0:T(4,128)(2,1)S(1)}, bf16[4,16384]{1,0:T(4,128)(2,1)S(1)}, u32[]{:S(2)}, u32[]{:S(2)}) collective-permute-start(bf16[4,16384]{1,0:T(4,128)(2,1)S(1)} %broadcast_select_fusion.15), channel_id=1, source_target_pairs={{0,8},{2,10},{4,12},{6,14},{8,0},{10,2},{12,4},{14,6},{16,24},{18,... | collective-permute-start | bytes 393224 | tf_op jit(solution)/shard_map/ppermute | solution.py:16
  364.1 12.3 %collective-permute-start.8 = (bf16[4,16384]{1,0:T(4,128)(2,1)S(1)}, bf16[4,16384]{1,0:T(4,128)(2,1)S(1)}, u32[]{:S(2)}, u32[]{:S(2)}) collective-permute-start(bf16[4,16384]{1,0:T(4,128)(2,1)S(1)} %broadcast_select_fusion.5), channel_id=1, source_target_pairs={{0,8},{2,10},{4,12},{6,14},{8,0},{10,2},{12,4},{14,6},{16,24},{18,... | collective-permute-start | bytes 393224 | tf_op jit(solution)/shard_map/ppermute | solution.py:16
  368.7 7.9 %collective-permute-start.15 = (bf16[4,16384]{1,0:T(4,128)(2,1)S(1)}, bf16[4,16384]{1,0:T(4,128)(2,1)S(1)}, u32[]{:S(2)}, u32[]{:S(2)}) collective-permute-start(bf16[4,16384]{1,0:T(4,128)(2,1)S(1)} %broadcast_select_fusion.16), channel_id=1, source_target_pairs={{0,16},{2,18},{4,20},{6,22},{8,24},{10,26},{12,28},{14,30},{16,0},... | collective-permute-start | bytes 393224 | tf_op jit(solution)/shard_map/ppermute | solution.py:16
  371.5 7.4 %collective-permute-start.21 = (bf16[4,16384]{1,0:T(4,128)(2,1)S(1)}, bf16[4,16384]{1,0:T(4,128)(2,1)S(1)}, u32[]{:S(2)}, u32[]{:S(2)}) collective-permute-start(bf16[4,16384]{1,0:T(4,128)(2,1)S(1)} %broadcast_select_fusion.6), channel_id=1, source_target_pairs={{0,16},{2,18},{4,20},{6,22},{8,24},{10,26},{12,28},{14,30},{16,0},... | collective-permute-start | bytes 393224 | tf_op jit(solution)/shard_map/ppermute | solution.py:16
  374.3 6.2 %collective-permute-start.3 = (bf16[4,16384]{1,0:T(4,128)(2,1)S(1)}, bf16[4,16384]{1,0:T(4,128)(2,1)S(1)}, u32[]{:S(2)}, u32[]{:S(2)}) collective-permute-start(bf16[4,16384]{1,0:T(4,128)(2,1)S(1)} %broadcast_select_fusion.17), channel_id=1, source_target_pairs={{0,16},{2,18},{4,20},{6,22},{8,24},{10,26},{12,28},{14,30},{16,0},... | collective-permute-start | bytes 393224 | tf_op jit(solution)/shard_map/ppermute | solution.py:16
  376.4 6.6 %collective-permute-start.9 = (bf16[4,16384]{1,0:T(4,128)(2,1)S(1)}, bf16[4,16384]{1,0:T(4,128)(2,1)S(1)}, u32[]{:S(2)}, u32[]{:S(2)}) collective-permute-start(bf16[4,16384]{1,0:T(4,128)(2,1)S(1)} %broadcast_select_fusion.7), channel_id=1, source_target_pairs={{0,16},{2,18},{4,20},{6,22},{8,24},{10,26},{12,28},{14,30},{16,0},... | collective-permute-start | bytes 393224 | tf_op jit(solution)/shard_map/ppermute | solution.py:16
  376.7 9.4 %collective-permute-start.16 = (bf16[4,16384]{1,0:T(4,128)(2,1)S(1)}, bf16[4,16384]{1,0:T(4,128)(2,1)S(1)}, u32[]{:S(2)}, u32[]{:S(2)}) collective-permute-start(bf16[4,16384]{1,0:T(4,128)(2,1)S(1)} %broadcast_select_fusion.18), channel_id=1, source_target_pairs={{0,32},{2,34},{4,36},{6,38},{8,40},{10,42},{12,44},{14,46},{16,48}... | collective-permute-start | bytes 393224 | tf_op jit(solution)/shard_map/ppermute | solution.py:16
  379.0 9.9 %collective-permute-start.22 = (bf16[4,16384]{1,0:T(4,128)(2,1)S(1)}, bf16[4,16384]{1,0:T(4,128)(2,1)S(1)}, u32[]{:S(2)}, u32[]{:S(2)}) collective-permute-start(bf16[4,16384]{1,0:T(4,128)(2,1)S(1)} %broadcast_select_fusion.8), channel_id=1, source_target_pairs={{0,32},{2,34},{4,36},{6,38},{8,40},{10,42},{12,44},{14,46},{16,48}... | collective-permute-start | bytes 393224 | tf_op jit(solution)/shard_map/ppermute | solution.py:16
  380.6 11.2 %collective-permute-start.4 = (bf16[4,16384]{1,0:T(4,128)(2,1)S(1)}, bf16[4,16384]{1,0:T(4,128)(2,1)S(1)}, u32[]{:S(2)}, u32[]{:S(2)}) collective-permute-start(bf16[4,16384]{1,0:T(4,128)(2,1)S(1)} %broadcast_select_fusion.19), channel_id=1, source_target_pairs={{0,32},{2,34},{4,36},{6,38},{8,40},{10,42},{12,44},{14,46},{16,48}... | collective-permute-start | bytes 393224 | tf_op jit(solution)/shard_map/ppermute | solution.py:16
  383.1 10.5 %collective-permute-start.10 = (bf16[4,16384]{1,0:T(4,128)(2,1)S(1)}, bf16[4,16384]{1,0:T(4,128)(2,1)S(1)}, u32[]{:S(2)}, u32[]{:S(2)}) collective-permute-start(bf16[4,16384]{1,0:T(4,128)(2,1)S(1)} %broadcast_select_fusion.9), channel_id=1, source_target_pairs={{0,32},{2,34},{4,36},{6,38},{8,40},{10,42},{12,44},{14,46},{16,48}... | collective-permute-start | bytes 393224 | tf_op jit(solution)/shard_map/ppermute | solution.py:16
  386.2 9.4 %collective-permute-start.17 = (bf16[4,16384]{1,0:T(4,128)(2,1)S(1)}, bf16[4,16384]{1,0:T(4,128)(2,1)S(1)}, u32[]{:S(2)}, u32[]{:S(2)}) collective-permute-start(bf16[4,16384]{1,0:T(4,128)(2,1)S(1)} %broadcast_select_fusion.20), channel_id=1, source_target_pairs={{0,64},{2,66},{4,68},{6,70},{8,72},{10,74},{12,76},{14,78},{16,80}... | collective-permute-start | bytes 393224 | tf_op jit(solution)/shard_map/ppermute | solution.py:16
  389.0 7.8 %collective-permute-start.23 = (bf16[4,16384]{1,0:T(4,128)(2,1)S(1)}, bf16[4,16384]{1,0:T(4,128)(2,1)S(1)}, u32[]{:S(2)}, u32[]{:S(2)}) collective-permute-start(bf16[4,16384]{1,0:T(4,128)(2,1)S(1)} %broadcast_select_fusion.10), channel_id=1, source_target_pairs={{0,64},{2,66},{4,68},{6,70},{8,72},{10,74},{12,76},{14,78},{16,80}... | collective-permute-start | bytes 393224 | tf_op jit(solution)/shard_map/ppermute | solution.py:16
  391.8 10.3 %collective-permute-start.5 = (bf16[4,16384]{1,0:T(4,128)(2,1)S(1)}, bf16[4,16384]{1,0:T(4,128)(2,1)S(1)}, u32[]{:S(2)}, u32[]{:S(2)}) collective-permute-start(bf16[4,16384]{1,0:T(4,128)(2,1)S(1)} %broadcast_select_fusion.21), channel_id=1, source_target_pairs={{0,64},{2,66},{4,68},{6,70},{8,72},{10,74},{12,76},{14,78},{16,80}... | collective-permute-start | bytes 393224 | tf_op jit(solution)/shard_map/ppermute | solution.py:16
  393.7 8.4 %collective-permute-start.11 = (bf16[4,16384]{1,0:T(4,128)(2,1)S(1)}, bf16[4,16384]{1,0:T(4,128)(2,1)S(1)}, u32[]{:S(2)}, u32[]{:S(2)}) collective-permute-start(bf16[4,16384]{1,0:T(4,128)(2,1)S(1)} %broadcast_select_fusion.11), channel_id=1, source_target_pairs={{0,64},{2,66},{4,68},{6,70},{8,72},{10,74},{12,76},{14,78},{16,80}... | collective-permute-start | bytes 393224 | tf_op jit(solution)/shard_map/ppermute | solution.py:16
  398.7 7.8 %all-to-all-start.3 = ((bf16[2,128,256]{2,1,0:T(8,128)(2,1)}), bf16[2,128,256]{2,1,0:T(8,128)(2,1)S(1)}, u32[]{:S(2)}, u32[]{:S(2)}) async-start(bf16[2,128,256]{2,1,0:T(8,128)(2,1)} %convert_element_type.74), calls=%async_computation.3 | async-start | bytes 262144 | tf_op jit(solution)/shard_map/all_to_all | solution.py:166
  406.5 7.8 %all-to-all-start.2 = ((bf16[2,128,256]{2,1,0:T(8,128)(2,1)}), bf16[2,128,256]{2,1,0:T(8,128)(2,1)S(1)}, u32[]{:S(2)}, u32[]{:S(2)}) async-start(bf16[2,128,256]{2,1,0:T(8,128)(2,1)} %convert_element_type.70), calls=%async_computation.2 | async-start | bytes 262144 | tf_op jit(solution)/shard_map/all_to_all | solution.py:165
  (5 other events, 7.8 us)
Sparse Core Ops, SparseCore 0:
  16.0 83.4 all-gather.4
  102.7 78.6 all-gather.2
where the time goes:
time: 424 us; the launch traced here: 422 us
  waiting for transfers between devices  173 us (41%)
  matrix products  88.8 us (21%)
  local copies, waits for them, and re-layouts  60.4 us (14%)
  starting transfers between devices  36.1 us (9%)
  other arithmetic  26.8 us (6%)
  between operations  21.2 us (5%)
  blocking collectives  15 us (4%)
    all_gather x1, waiting for transfers between devices, body(): lax.all_gather(values_local, 'ctx', axis=0, tiled=True)  81.9 us
    all_gather x1, waiting for transfers between devices, body(): lax.all_gather(keys_local, 'ctx', axis=0, tiled=True)  66.7 us
    ppermute x24, starting transfers between devices, from_partner(): return lax.ppermute(value, axis, pairs)  29.3 us
    sub x4, matrix products, one_block(): exp_scores = jnp.exp(scores - row_max)  18.8 us
    ppermute x24, waiting for transfers between devices, from_partner(): return lax.ppermute(value, axis, pairs)  18.5 us
    dot_general x4, matrix products, one_block(): jnp.einsum('qgrd,kgd->grqk', grad_block, picked_values, preferred_element...  14.5 us
    convert_element_type x4, other arithmetic, one_block(): prob_low = prob_full.astype(jnp.bfloat16)  12.9 us
    dot_general x4, matrix products, one_block(): jnp.einsum('grqk,qgrd->kgd', prob_low, grad_block, preferred_element_type...  12.5 us
  transfers between devices with their start and end apart: 28, of which 15 were waited for; matrix products, arithmetic and copies ran while one was open for 2% of the time, Pallas kernels for 0%

commit v1 on v0

--- a/solution.py
+++ b/solution.py
@@ -50,9 +50,16 @@
     mask_first = partners[0, 0]
     mask_second = partners[1, 0]
     bit_total = lax.axis_size("ctx").bit_length() - 1
+
+    def bind_links(piece_in, net_axis, along_dim):
+        side_arr = jnp.stack([piece_in for _ in range(lax.axis_size(net_axis))])
+        block_last = lax.all_to_all(side_arr, net_axis, 0, 0)
+        known = jnp.concatenate(block_last, axis=along_dim)
+        return known
+
     every_key, every_value = (
         lax.all_gather(keys_local, "ctx", axis=0, tiled=True),
-        lax.all_gather(values_local, "ctx", axis=0, tiled=True),
+        bind_links(values_local, "ctx", 0),
     )
     own_index = lax.axis_index("ctx")
 

time: 424 us -> 447 us (1.054)
  local copies, waits for them, and re-layouts: 60.4 us -> 92.7 us
  matrix products: 88.8 us -> 76.3 us
  starting transfers between devices: 36.1 us -> 48 us
  waiting for transfers between devices: 173 us -> 165 us
    all_to_all x0 -> x1, waiting for transfers between devices: none -> 99.2 us  [bind_links(): block_last = lax.all_to_all(side_arr, net_axis, 0, 0)]
    all_gather x1 -> x0, waiting for transfers between devices: 81.9 us -> none  [body(): lax.all_gather(values_local, 'ctx', axis=0, tiled=True)]
    all_gather x1, waiting for transfers between devices: 66.7 us -> 41.6 us  [body(): lax.all_gather(keys_local, 'ctx', axis=0, tiled=True)]
    all_to_all x0 -> x1, starting transfers between devices: none -> 11.9 us  [bind_links(): block_last = lax.all_to_all(side_arr, net_axis, 0, 0)]
    while x64 -> x104, local copies, waits for them, and re-layouts: 9.47 us -> 21.3 us
    reshape x4, local copies, waits for them, and re-layouts: 2.52 us -> 11 us  [one_block(): key_part = jnp.einsum('grqk,qgrd->kgd', grad_s, query_block, preferred_el...]
    dot_general x4, matrix products: 14.5 us -> 6.43 us  [one_block(): jnp.einsum('qgrd,kgd->grqk', grad_block, picked_values, preferred_element...]
    dot_general x4, matrix products: 10.7 us -> 3.49 us  [one_block(): jnp.dot(one_hot.T, value_part, precision=lax.Precision.HIGHEST, preferred...]
  transfers between devices with their start and end apart: 28 -> 28, of which waited for: 15 -> 15; matrix products, arithmetic and copies ran while one was open for 2% -> 3% of each run, Pallas kernels for 0% -> 0%
where the time goes in v1:
time: 447 us; the launch traced here: 445 us
  waiting for transfers between devices  165 us (37%)
  local copies, waits for them, and re-layouts  92.7 us (21%)
  matrix products  76.3 us (17%)
  starting transfers between devices  48 us (11%)
  other arithmetic  25.9 us (6%)
  between operations  21.1 us (5%)
  blocking collectives  14.4 us (3%)
    all_to_all x1, waiting for transfers between devices, bind_links(): block_last = lax.all_to_all(side_arr, net_axis, 0, 0)  99.2 us
    all_gather x1, waiting for transfers between devices, body(): lax.all_gather(keys_local, 'ctx', axis=0, tiled=True)  41.6 us
    ppermute x24, starting transfers between devices, from_partner(): return lax.ppermute(value, axis, pairs)  29.3 us
    while x104, local copies, waits for them, and re-layouts  21.3 us
    sub x4, matrix products, one_block(): exp_scores = jnp.exp(scores - row_max)  18.8 us
    ppermute x24, waiting for transfers between devices, from_partner(): return lax.ppermute(value, axis, pairs)  18.5 us
    convert_element_type x4, other arithmetic, one_block(): prob_low = prob_full.astype(jnp.bfloat16)  12.9 us
    dot_general x4, matrix products, one_block(): jnp.dot(one_hot.T, key_part, precision=lax.Precision.HIGHEST, preferred_e...  12.8 us
  transfers between devices with their start and end apart: 28, of which 15 were waited for; matrix products, arithmetic and copies ran while one was open for 3% of the time, Pallas kernels for 0%

profile of v1, /device:TPU:0, one launch (start us, length us, event | category | flops | bytes accessed | tf_op | source)
XLA Modules:
  0.0 444.6 jit_solution(8164516251626761168)
XLA Ops:
  8.4 7.5 %all_to_all.75 = bf16[128,2,256]{2,0,1:T(8,128)(2,1)} all-to-all(bf16[128,2,256]{2,0,1:T(8,128)(2,1)S(1)} %copy.61), channel_id=1, replica_groups=mesh['ctx'=64,'head'=2] {'head'}, dimensions={1} | all-to-all | bytes 262144 | tf_op jit(solution)/shard_map/all_to_all | solution.py:47
  17.1 6.8 %all_to_all.76 = bf16[128,2,256]{2,0,1:T(8,128)(2,1)S(1)} all-to-all(bf16[128,2,256]{2,0,1:T(8,128)(2,1)S(1)} %copy.59), channel_id=1, replica_groups=mesh['ctx'=64,'head'=2] {'head'}, dimensions={1} | all-to-all | bytes 262144 | tf_op jit(solution)/shard_map/all_to_all | solution.py:48
  23.9 4.3 stack.2
  28.2 11.9 %all-to-all-start.1 = ((bf16[64,256,256]{2,1,0:T(8,128)(2,1)}), bf16[64,256,256]{2,1,0:T(8,128)(2,1)}, u32[]{:S(2)}, u32[]{:S(2)}) async-start(bf16[64,256,256]{2,1,0:T(8,128)(2,1)} %stack.2), calls=%async_computation.1 | async-start | bytes 16777216 | tf_op jit(solution)/shard_map/all_to_all | solution.py:56
  47.6 99.2 %all-to-all-done.1 = bf16[64,256,256]{2,1,0:T(8,128)(2,1)} async-done(((bf16[64,256,256]{2,1,0:T(8,128)(2,1)}), bf16[64,256,256]{2,1,0:T(8,128)(2,1)}, u32[]{:S(2)}, u32[]{:S(2)}) %all-to-all-start.1) | async-done | bytes 8388640 | tf_op jit(solution)/shard_map/all_to_all | solution.py:56
  146.8 41.6 %all-gather.2.cloned.1.call-done = bf16[16384,256]{1,0:T(8,128)(2,1)} async-done(((bf16[256,256]{1,0:T(8,128)(2,1)}), bf16[16384,256]{1,0:T(8,128)(2,1)}) %all-gather.2.cloned.1.call-update) | async-done | bytes 8388624 | tf_op jit(solution)/shard_map/all_gather | solution.py:61
  194.5 172.6 %while.20 = (s32[]{:T(128)}, bf16[256,4096]{1,0:T(8,128)(2,1)}, bf16[256,4096]{1,0:T(8,128)(2,1)}, f32[12,16384]{1,0:T(8,128)}, f32[12,16384]{1,0:T(8,128)}, /*i...) while((s32[]{:T(128)}, bf16[256,4096]{1,0:T(8,128)(2,1)}, ...), condition=%wide.region_3.5_spmd.clone, body=%wide.region_0.4_spmd.clone.sunk | while | flops 2491023616 | bytes 112244064 | solution.py:145
  195.7 2.3 gather_fusion
  198.0 2.3 gather_fusion.1
  202.5 4.7 %fusion.96 = (f32[2,16,64]{2,1,0:T(8,128)S(1)}, f32[2,16,64,768]{3,2,1,0:T(8,128)}) fusion(bf16[64,2,16,128]{3,2,1,0:T(8,128)(2,1)S(1)} %bitcast.141, bf16[768,2,128,1]{2,1,0,3:T(2,128)(2,1)S(1)} %bitcast.139), kind=kOutput, calls=%fused_computation.82.clone.1 | convolution fusion | flops 407372544 | bytes 7217152 | tf_op jit(solution)/shard_map/while/body/eval_jaxpr/sub | solution.py:99
  207.2 3.2 fusion.97
  219.3 3.1 fusion.100
  224.5 2.8 reshape.157
  227.3 3.0 convolution_add_fusion.4
  230.3 3.1 fusion.101
  238.6 2.3 gather_fusion
  241.0 2.3 gather_fusion.1
  245.4 4.7 %fusion.96 = (f32[2,16,64]{2,1,0:T(8,128)S(1)}, f32[2,16,64,768]{3,2,1,0:T(8,128)}) fusion(bf16[64,2,16,128]{3,2,1,0:T(8,128)(2,1)S(1)} %bitcast.141, bf16[768,2,128,1]{2,1,0,3:T(2,128)(2,1)S(1)} %bitcast.139), kind=kOutput, calls=%fused_computation.82.clone.1 | convolution fusion | flops 407372544 | bytes 7217152 | tf_op jit(solution)/shard_map/while/body/eval_jaxpr/sub | solution.py:99
  250.1 3.2 fusion.97
  262.2 3.1 fusion.100
  267.5 2.8 reshape.157
  270.2 3.3 convolution_add_fusion.4
  273.5 3.1 fusion.101
  281.9 2.3 gather_fusion
  284.2 2.3 gather_fusion.1
  288.7 4.7 %fusion.96 = (f32[2,16,64]{2,1,0:T(8,128)S(1)}, f32[2,16,64,768]{3,2,1,0:T(8,128)}) fusion(bf16[64,2,16,128]{3,2,1,0:T(8,128)(2,1)S(1)} %bitcast.141, bf16[768,2,128,1]{2,1,0,3:T(2,128)(2,1)S(1)} %bitcast.139), kind=kOutput, calls=%fused_computation.82.clone.1 | convolution fusion | flops 407372544 | bytes 7217152 | tf_op jit(solution)/shard_map/while/body/eval_jaxpr/sub | solution.py:99
  293.4 3.2 fusion.97
  305.5 3.1 fusion.100
  310.7 2.8 reshape.157
  313.5 3.3 convolution_add_fusion.4
  316.7 3.1 fusion.101
  327.4 2.3 gather_fusion.1
  331.9 4.7 %fusion.96 = (f32[2,16,64]{2,1,0:T(8,128)S(1)}, f32[2,16,64,768]{3,2,1,0:T(8,128)}) fusion(bf16[64,2,16,128]{3,2,1,0:T(8,128)(2,1)S(1)} %bitcast.141, bf16[768,2,128,1]{2,1,0,3:T(2,128)(2,1)S(1)} %bitcast.139), kind=kOutput, calls=%fused_computation.82.clone.1 | convolution fusion | flops 407372544 | bytes 7217152 | tf_op jit(solution)/shard_map/while/body/eval_jaxpr/sub | solution.py:99
  336.6 3.2 fusion.97
  348.7 3.1 fusion.100
  353.9 2.8 reshape.157
  356.7 3.3 convolution_add_fusion.4
  360.0 3.1 fusion.101
  377.8 3.1 collective-permute-start.14
  380.9 2.7 collective-permute-start.20
  383.7 2.7 collective-permute-start.2
  386.6 2.7 collective-permute-start.8
  391.4 2.5 collective-permute-done.20
  394.2 2.5 collective-permute-done.2
  421.2 3.4 all-to-all-start.4
  426.5 2.5 all-to-all-done.4
  429.0 3.4 all-to-all-start.3
  433.3 3.6 all-to-all-done.3
  (257 shorter events, 125.0 us)
Async XLA Ops:
  7.2 181.2 %all-gather.2.cloned.1.call-start = ((), (), s32[]{:S(2)}) async-start(), calls=%async_computation.5 | async-start | bytes 8519680 | tf_op jit(solution)/shard_map/all_gather | solution.py:61
  28.2 11.9 %copy-start.12 = (s32[2,64]{1,0:T(2,128)S(1)}, s32[2,64]{1,0:T(2,128)}, u32[]{:S(2)}) copy-start(s32[2,64]{1,0:T(2,128)} %param.15) | copy-start | bytes 1540
  28.2 161.3 %copy-start.9 = (bf16[128,2,256]{2,0,1:T(8,128)(2,1)S(1)}, bf16[128,2,256]{2,0,1:T(8,128)(2,1)}, u32[]{:S(2)}) copy-start(bf16[128,2,256]{2,0,1:T(8,128)(2,1)} %all_to_all.75) | copy-start | bytes 393220
  28.2 118.6 %all-to-all-start.1 = ((bf16[64,256,256]{2,1,0:T(8,128)(2,1)}), bf16[64,256,256]{2,1,0:T(8,128)(2,1)}, u32[]{:S(2)}, u32[]{:S(2)}) async-start(bf16[64,256,256]{2,1,0:T(8,128)(2,1)} %stack.2), calls=%async_computation.1 | async-start | bytes 16777216 | tf_op jit(solution)/shard_map/all_to_all | solution.py:56
  201.2 6.1 %copy-start.5 = (bf16[12,64,2,128]{3,2,1,0:T(2,128)(2,1)}, bf16[12,64,2,128]{3,2,1,0:T(2,128)(2,1)S(1)}, u32[]{:S(2)}) copy-start(bf16[12,64,2,128]{3,2,1,0:T(2,128)(2,1)S(1)} %get-tuple-element.354) | copy-start | bytes 1179652 | tf_op jit(solution)/shard_map/while
  202.5 4.7 %copy-start.7 = (bf16[8,8,32,128]{3,2,1,0:T(8,128)(2,1)}, bf16[8,8,32,128]{3,2,1,0:T(8,128)(2,1)S(1)}, u32[]{:S(2)}) copy-start(bf16[8,8,32,128]{3,2,1,0:T(8,128)(2,1)S(1)} %copy.158) | copy-start | bytes 1572868 | tf_op jit(solution)/shard_map/while
  216.2 3.1 copy-start.8
  219.3 8.0 %copy-start.11 = (s32[12]{0:T(128)S(1)}, s32[12]{0:T(128)}, u32[]{:S(2)}) copy-start(s32[12]{0:T(128)} %copy-done.10) | copy-start | bytes 148 | tf_op jit(solution)/shard_map/while
  244.1 6.1 %copy-start.5 = (bf16[12,64,2,128]{3,2,1,0:T(2,128)(2,1)}, bf16[12,64,2,128]{3,2,1,0:T(2,128)(2,1)S(1)}, u32[]{:S(2)}) copy-start(bf16[12,64,2,128]{3,2,1,0:T(2,128)(2,1)S(1)} %get-tuple-element.354) | copy-start | bytes 1179652 | tf_op jit(solution)/shard_map/while
  245.4 4.7 %copy-start.7 = (bf16[8,8,32,128]{3,2,1,0:T(8,128)(2,1)}, bf16[8,8,32,128]{3,2,1,0:T(8,128)(2,1)S(1)}, u32[]{:S(2)}) copy-start(bf16[8,8,32,128]{3,2,1,0:T(8,128)(2,1)S(1)} %copy.158) | copy-start | bytes 1572868 | tf_op jit(solution)/shard_map/while
  259.2 3.1 copy-start.8
  262.2 8.0 %copy-start.11 = (s32[12]{0:T(128)S(1)}, s32[12]{0:T(128)}, u32[]{:S(2)}) copy-start(s32[12]{0:T(128)} %copy-done.10) | copy-start | bytes 148 | tf_op jit(solution)/shard_map/while
  270.2 3.3 copy-start.2
  287.3 6.1 %copy-start.5 = (bf16[12,64,2,128]{3,2,1,0:T(2,128)(2,1)}, bf16[12,64,2,128]{3,2,1,0:T(2,128)(2,1)S(1)}, u32[]{:S(2)}) copy-start(bf16[12,64,2,128]{3,2,1,0:T(2,128)(2,1)S(1)} %get-tuple-element.354) | copy-start | bytes 1179652 | tf_op jit(solution)/shard_map/while
  288.7 4.7 %copy-start.7 = (bf16[8,8,32,128]{3,2,1,0:T(8,128)(2,1)}, bf16[8,8,32,128]{3,2,1,0:T(8,128)(2,1)S(1)}, u32[]{:S(2)}) copy-start(bf16[8,8,32,128]{3,2,1,0:T(8,128)(2,1)S(1)} %copy.158) | copy-start | bytes 1572868 | tf_op jit(solution)/shard_map/while
  305.5 8.0 %copy-start.11 = (s32[12]{0:T(128)S(1)}, s32[12]{0:T(128)}, u32[]{:S(2)}) copy-start(s32[12]{0:T(128)} %copy-done.10) | copy-start | bytes 148 | tf_op jit(solution)/shard_map/while
  313.4 3.3 copy-start.2
  330.5 6.1 %copy-start.5 = (bf16[12,64,2,128]{3,2,1,0:T(2,128)(2,1)}, bf16[12,64,2,128]{3,2,1,0:T(2,128)(2,1)S(1)}, u32[]{:S(2)}) copy-start(bf16[12,64,2,128]{3,2,1,0:T(2,128)(2,1)S(1)} %get-tuple-element.354) | copy-start | bytes 1179652 | tf_op jit(solution)/shard_map/while
  331.9 4.7 %copy-start.7 = (bf16[8,8,32,128]{3,2,1,0:T(8,128)(2,1)}, bf16[8,8,32,128]{3,2,1,0:T(8,128)(2,1)S(1)}, u32[]{:S(2)}) copy-start(bf16[8,8,32,128]{3,2,1,0:T(8,128)(2,1)S(1)} %copy.158) | copy-start | bytes 1572868 | tf_op jit(solution)/shard_map/while
  345.6 3.1 copy-start.8
  348.7 8.0 %copy-start.11 = (s32[12]{0:T(128)S(1)}, s32[12]{0:T(128)}, u32[]{:S(2)}) copy-start(s32[12]{0:T(128)} %copy-done.10) | copy-start | bytes 148 | tf_op jit(solution)/shard_map/while
  356.7 3.3 copy-start.2
  368.5 2.6 collective-permute-start.12
  368.9 2.3 collective-permute-start.18
  370.5 2.9 collective-permute-start
  370.8 2.6 collective-permute-start.6
  371.3 6.4 %collective-permute-start.13 = (bf16[4,16384]{1,0:T(4,128)(2,1)S(1)}, bf16[4,16384]{1,0:T(4,128)(2,1)S(1)}, u32[]{:S(2)}, u32[]{:S(2)}) collective-permute-start(bf16[4,16384]{1,0:T(4,128)(2,1)S(1)} %get-tuple-element.269), channel_id=1, source_target_pairs={{0,4},{2,6},{4,0},{6,2},{8,12},{10,14},{12,8},{14,10},{16,20},{18,... | collective-permute-start | bytes 393224 | tf_op jit(solution)/shard_map/ppermute | solution.py:16
  372.8 8.0 %collective-permute-start.19 = (bf16[4,16384]{1,0:T(4,128)(2,1)S(1)}, bf16[4,16384]{1,0:T(4,128)(2,1)S(1)}, u32[]{:S(2)}, u32[]{:S(2)}) collective-permute-start(bf16[4,16384]{1,0:T(4,128)(2,1)S(1)} %get-tuple-element.270), channel_id=1, source_target_pairs={{0,4},{2,6},{4,0},{6,2},{8,12},{10,14},{12,8},{14,10},{16,20},{18,... | collective-permute-start | bytes 393224 | tf_op jit(solution)/shard_map/ppermute | solution.py:16
  373.6 10.1 %collective-permute-start.1 = (bf16[4,16384]{1,0:T(4,128)(2,1)S(1)}, bf16[4,16384]{1,0:T(4,128)(2,1)S(1)}, u32[]{:S(2)}, u32[]{:S(2)}) collective-permute-start(bf16[4,16384]{1,0:T(4,128)(2,1)S(1)} %get-tuple-element.273), channel_id=1, source_target_pairs={{0,4},{2,6},{4,0},{6,2},{8,12},{10,14},{12,8},{14,10},{16,20},{18,... | collective-permute-start | bytes 393224 | tf_op jit(solution)/shard_map/ppermute | solution.py:16
  375.1 11.3 %collective-permute-start.7 = (bf16[4,16384]{1,0:T(4,128)(2,1)S(1)}, bf16[4,16384]{1,0:T(4,128)(2,1)S(1)}, u32[]{:S(2)}, u32[]{:S(2)}) collective-permute-start(bf16[4,16384]{1,0:T(4,128)(2,1)S(1)} %get-tuple-element.274), channel_id=1, source_target_pairs={{0,4},{2,6},{4,0},{6,2},{8,12},{10,14},{12,8},{14,10},{16,20},{18,... | collective-permute-start | bytes 393224 | tf_op jit(solution)/shard_map/ppermute | solution.py:16
  377.8 13.3 %collective-permute-start.14 = (bf16[4,16384]{1,0:T(4,128)(2,1)S(1)}, bf16[4,16384]{1,0:T(4,128)(2,1)S(1)}, u32[]{:S(2)}, u32[]{:S(2)}) collective-permute-start(bf16[4,16384]{1,0:T(4,128)(2,1)S(1)} %broadcast_select_fusion.14), channel_id=1, source_target_pairs={{0,8},{2,10},{4,12},{6,14},{8,0},{10,2},{12,4},{14,6},{16,24},{18,... | collective-permute-start | bytes 393224 | tf_op jit(solution)/shard_map/ppermute | solution.py:16
  380.9 13.0 %collective-permute-start.20 = (bf16[4,16384]{1,0:T(4,128)(2,1)S(1)}, bf16[4,16384]{1,0:T(4,128)(2,1)S(1)}, u32[]{:S(2)}, u32[]{:S(2)}) collective-permute-start(bf16[4,16384]{1,0:T(4,128)(2,1)S(1)} %broadcast_select_fusion.4), channel_id=1, source_target_pairs={{0,8},{2,10},{4,12},{6,14},{8,0},{10,2},{12,4},{14,6},{16,24},{18,... | collective-permute-start | bytes 393224 | tf_op jit(solution)/shard_map/ppermute | solution.py:16
  383.7 13.0 %collective-permute-start.2 = (bf16[4,16384]{1,0:T(4,128)(2,1)S(1)}, bf16[4,16384]{1,0:T(4,128)(2,1)S(1)}, u32[]{:S(2)}, u32[]{:S(2)}) collective-permute-start(bf16[4,16384]{1,0:T(4,128)(2,1)S(1)} %broadcast_select_fusion.15), channel_id=1, source_target_pairs={{0,8},{2,10},{4,12},{6,14},{8,0},{10,2},{12,4},{14,6},{16,24},{18,... | collective-permute-start | bytes 393224 | tf_op jit(solution)/shard_map/ppermute | solution.py:16
  386.6 12.3 %collective-permute-start.8 = (bf16[4,16384]{1,0:T(4,128)(2,1)S(1)}, bf16[4,16384]{1,0:T(4,128)(2,1)S(1)}, u32[]{:S(2)}, u32[]{:S(2)}) collective-permute-start(bf16[4,16384]{1,0:T(4,128)(2,1)S(1)} %broadcast_select_fusion.5), channel_id=1, source_target_pairs={{0,8},{2,10},{4,12},{6,14},{8,0},{10,2},{12,4},{14,6},{16,24},{18,... | collective-permute-start | bytes 393224 | tf_op jit(solution)/shard_map/ppermute | solution.py:16
  391.2 7.9 %collective-permute-start.15 = (bf16[4,16384]{1,0:T(4,128)(2,1)S(1)}, bf16[4,16384]{1,0:T(4,128)(2,1)S(1)}, u32[]{:S(2)}, u32[]{:S(2)}) collective-permute-start(bf16[4,16384]{1,0:T(4,128)(2,1)S(1)} %broadcast_select_fusion.16), channel_id=1, source_target_pairs={{0,16},{2,18},{4,20},{6,22},{8,24},{10,26},{12,28},{14,30},{16,0},... | collective-permute-start | bytes 393224 | tf_op jit(solution)/shard_map/ppermute | solution.py:16
  394.0 7.4 %collective-permute-start.21 = (bf16[4,16384]{1,0:T(4,128)(2,1)S(1)}, bf16[4,16384]{1,0:T(4,128)(2,1)S(1)}, u32[]{:S(2)}, u32[]{:S(2)}) collective-permute-start(bf16[4,16384]{1,0:T(4,128)(2,1)S(1)} %broadcast_select_fusion.6), channel_id=1, source_target_pairs={{0,16},{2,18},{4,20},{6,22},{8,24},{10,26},{12,28},{14,30},{16,0},... | collective-permute-start | bytes 393224 | tf_op jit(solution)/shard_map/ppermute | solution.py:16
  396.8 6.2 %collective-permute-start.3 = (bf16[4,16384]{1,0:T(4,128)(2,1)S(1)}, bf16[4,16384]{1,0:T(4,128)(2,1)S(1)}, u32[]{:S(2)}, u32[]{:S(2)}) collective-permute-start(bf16[4,16384]{1,0:T(4,128)(2,1)S(1)} %broadcast_select_fusion.17), channel_id=1, source_target_pairs={{0,16},{2,18},{4,20},{6,22},{8,24},{10,26},{12,28},{14,30},{16,0},... | collective-permute-start | bytes 393224 | tf_op jit(solution)/shard_map/ppermute | solution.py:16
  398.9 6.6 %collective-permute-start.9 = (bf16[4,16384]{1,0:T(4,128)(2,1)S(1)}, bf16[4,16384]{1,0:T(4,128)(2,1)S(1)}, u32[]{:S(2)}, u32[]{:S(2)}) collective-permute-start(bf16[4,16384]{1,0:T(4,128)(2,1)S(1)} %broadcast_select_fusion.7), channel_id=1, source_target_pairs={{0,16},{2,18},{4,20},{6,22},{8,24},{10,26},{12,28},{14,30},{16,0},... | collective-permute-start | bytes 393224 | tf_op jit(solution)/shard_map/ppermute | solution.py:16
  399.2 9.4 %collective-permute-start.16 = (bf16[4,16384]{1,0:T(4,128)(2,1)S(1)}, bf16[4,16384]{1,0:T(4,128)(2,1)S(1)}, u32[]{:S(2)}, u32[]{:S(2)}) collective-permute-start(bf16[4,16384]{1,0:T(4,128)(2,1)S(1)} %broadcast_select_fusion.18), channel_id=1, source_target_pairs={{0,32},{2,34},{4,36},{6,38},{8,40},{10,42},{12,44},{14,46},{16,48}... | collective-permute-start | bytes 393224 | tf_op jit(solution)/shard_map/ppermute | solution.py:16
  401.4 9.9 %collective-permute-start.22 = (bf16[4,16384]{1,0:T(4,128)(2,1)S(1)}, bf16[4,16384]{1,0:T(4,128)(2,1)S(1)}, u32[]{:S(2)}, u32[]{:S(2)}) collective-permute-start(bf16[4,16384]{1,0:T(4,128)(2,1)S(1)} %broadcast_select_fusion.8), channel_id=1, source_target_pairs={{0,32},{2,34},{4,36},{6,38},{8,40},{10,42},{12,44},{14,46},{16,48}... | collective-permute-start | bytes 393224 | tf_op jit(solution)/shard_map/ppermute | solution.py:16
  403.0 11.2 %collective-permute-start.4 = (bf16[4,16384]{1,0:T(4,128)(2,1)S(1)}, bf16[4,16384]{1,0:T(4,128)(2,1)S(1)}, u32[]{:S(2)}, u32[]{:S(2)}) collective-permute-start(bf16[4,16384]{1,0:T(4,128)(2,1)S(1)} %broadcast_select_fusion.19), channel_id=1, source_target_pairs={{0,32},{2,34},{4,36},{6,38},{8,40},{10,42},{12,44},{14,46},{16,48}... | collective-permute-start | bytes 393224 | tf_op jit(solution)/shard_map/ppermute | solution.py:16
  405.6 10.5 %collective-permute-start.10 = (bf16[4,16384]{1,0:T(4,128)(2,1)S(1)}, bf16[4,16384]{1,0:T(4,128)(2,1)S(1)}, u32[]{:S(2)}, u32[]{:S(2)}) collective-permute-start(bf16[4,16384]{1,0:T(4,128)(2,1)S(1)} %broadcast_select_fusion.9), channel_id=1, source_target_pairs={{0,32},{2,34},{4,36},{6,38},{8,40},{10,42},{12,44},{14,46},{16,48}... | collective-permute-start | bytes 393224 | tf_op jit(solution)/shard_map/ppermute | solution.py:16
  408.6 9.4 %collective-permute-start.17 = (bf16[4,16384]{1,0:T(4,128)(2,1)S(1)}, bf16[4,16384]{1,0:T(4,128)(2,1)S(1)}, u32[]{:S(2)}, u32[]{:S(2)}) collective-permute-start(bf16[4,16384]{1,0:T(4,128)(2,1)S(1)} %broadcast_select_fusion.20), channel_id=1, source_target_pairs={{0,64},{2,66},{4,68},{6,70},{8,72},{10,74},{12,76},{14,78},{16,80}... | collective-permute-start | bytes 393224 | tf_op jit(solution)/shard_map/ppermute | solution.py:16
  411.4 7.8 %collective-permute-start.23 = (bf16[4,16384]{1,0:T(4,128)(2,1)S(1)}, bf16[4,16384]{1,0:T(4,128)(2,1)S(1)}, u32[]{:S(2)}, u32[]{:S(2)}) collective-permute-start(bf16[4,16384]{1,0:T(4,128)(2,1)S(1)} %broadcast_select_fusion.10), channel_id=1, source_target_pairs={{0,64},{2,66},{4,68},{6,70},{8,72},{10,74},{12,76},{14,78},{16,80}... | collective-permute-start | bytes 393224 | tf_op jit(solution)/shard_map/ppermute | solution.py:16
  414.2 10.3 %collective-permute-start.5 = (bf16[4,16384]{1,0:T(4,128)(2,1)S(1)}, bf16[4,16384]{1,0:T(4,128)(2,1)S(1)}, u32[]{:S(2)}, u32[]{:S(2)}) collective-permute-start(bf16[4,16384]{1,0:T(4,128)(2,1)S(1)} %broadcast_select_fusion.21), channel_id=1, source_target_pairs={{0,64},{2,66},{4,68},{6,70},{8,72},{10,74},{12,76},{14,78},{16,80}... | collective-permute-start | bytes 393224 | tf_op jit(solution)/shard_map/ppermute | solution.py:16
  416.2 8.4 %collective-permute-start.11 = (bf16[4,16384]{1,0:T(4,128)(2,1)S(1)}, bf16[4,16384]{1,0:T(4,128)(2,1)S(1)}, u32[]{:S(2)}, u32[]{:S(2)}) collective-permute-start(bf16[4,16384]{1,0:T(4,128)(2,1)S(1)} %broadcast_select_fusion.11), channel_id=1, source_target_pairs={{0,64},{2,66},{4,68},{6,70},{8,72},{10,74},{12,76},{14,78},{16,80}... | collective-permute-start | bytes 393224 | tf_op jit(solution)/shard_map/ppermute | solution.py:16
  421.2 7.8 %all-to-all-start.4 = ((bf16[2,128,256]{2,1,0:T(8,128)(2,1)}), bf16[2,128,256]{2,1,0:T(8,128)(2,1)S(1)}, u32[]{:S(2)}, u32[]{:S(2)}) async-start(bf16[2,128,256]{2,1,0:T(8,128)(2,1)} %convert_element_type.74), calls=%async_computation.4 | async-start | bytes 262144 | tf_op jit(solution)/shard_map/all_to_all | solution.py:173
  429.0 7.8 %all-to-all-start.3 = ((bf16[2,128,256]{2,1,0:T(8,128)(2,1)}), bf16[2,128,256]{2,1,0:T(8,128)(2,1)S(1)}, u32[]{:S(2)}, u32[]{:S(2)}) async-start(bf16[2,128,256]{2,1,0:T(8,128)(2,1)} %convert_element_type.70), calls=%async_computation.3 | async-start | bytes 262144 | tf_op jit(solution)/shard_map/all_to_all | solution.py:172
  (26 other events, 45.3 us)
Sparse Core Ops, SparseCore 0:
  16.0 172.3 all-gather.1
